TPU v7x, 256 devices: a whole 4x4x8 slice. The times are simulated.
256 devices in a mesh: row: 32 (over y, x, core), col: 8 (over z).
Axes of the slice: x: 4, y: 4, z: 8, core: 2. Of those that a mesh axis runs over, the one named last changes fastest.
Arguments:
- matrix: float32 [98304, 4096], P('row', 'col'), may hold values from -6 to 6
Outputs:
- top_rows: float32 [4096, 256], P(('col', 'row'))
- remainder: float32 [98304, 4096], P('row', 'col')
All inputs are finite; a program needn't handle non-finite values.
Results may differ from a plain program's by a relative error of at most 0.00013.
Values sent between devices are 32-bit elements; how exact they have to be, the bound alone decides.
A program may use at most 64 MiB of HBM per device.

v0:
```python
import jax
import jax.numpy as jnp
from jax import lax
from jax.sharding import PartitionSpec as P

PANEL = 256


def broadcast(block, axis, owner):
    block = jnp.where(lax.axis_index(axis) == owner, block, jnp.zeros_like(block))
    return lax.psum(block, axis)


def gram_total(panel_cols):
    local_gram = lax.dot_general(
        panel_cols,
        panel_cols,
        (((0,), (0,)), ((), ())),
        precision=lax.Precision.HIGHEST,
        preferred_element_type=jnp.float32,
    )
    return lax.psum(local_gram, "row")


def shards(matrix):
    highest = lax.Precision.HIGHEST
    own_panel = matrix[:, :PANEL]
    lower_factor = jnp.linalg.cholesky(gram_total(own_panel))
    panel_cols, lower_factor = (broadcast(own_panel, "col", 0), broadcast(lower_factor, "col", 0))
    column_block = matrix
    products = lax.psum_scatter(
        lax.dot_general(
            column_block,
            panel_cols,
            (((0,), (0,)), ((), ())),
            precision=highest,
            preferred_element_type=jnp.float32,
        ),
        "row",
        scatter_dimension=0,
        tiled=True,
    )
    top_rows = lax.linalg.triangular_solve(
        lower_factor, products, left_side=False, lower=True, transpose_a=True
    )
    coeffs = lax.linalg.triangular_solve(lower_factor, top_rows, left_side=False, lower=True)
    column_block = matrix
    remainder = column_block - lax.dot_general(
        panel_cols,
        lax.all_gather(coeffs, "row", axis=0, tiled=True),
        (((1,), (1,)), ((), ())),
        precision=highest,
        preferred_element_type=jnp.float32,
    )
    return (top_rows, remainder)


def solution(mesh):
    return jax.shard_map(
        shards,
        mesh=mesh,
        in_specs=(P("row", "col"),),
        out_specs=(P(("col", "row"), None), P("row", "col")),
        check_vma=False,
    )
```

profile of v0, /device:TPU:33, one launch (start us, length us, event | category | flops | bytes accessed | tf_op | source)
XLA Modules:
  0.0 409.8 jit_solution(11529678995246782062)
XLA Ops:
  7.2 8.7 %fusion = f32[256,256]{0,1:T(8,128)} fusion(f32[3072,512]{1,0:T(8,128)} %param.1), kind=kOutput, calls=%fused_computation.3 | convolution fusion | flops 2415919104 | bytes 3407872 | tf_op jit(solution)/shard_map/dot_general | solution.py:15
  16.1 3.8 slice_select_fusion
  19.9 111.1 %all-reduce.5.cloned.1.call-done = f32[256,256]{0,1:T(8,128)} async-done(((f32[256,256]{0,1:T(8,128)}), f32[256,256]{0,1:T(8,128)}) %all-reduce.5.cloned.1.call-update) | async-done | bytes 262160 | tf_op jit(solution)/shard_map/psum | solution.py:22
  131.0 1.1 copy.6
  132.1 1.0 fusion.2
  133.1 11.7 %cholesky.50 = f32[128,128]{1,0:T(8,128)S(1)} custom-call(f32[128,128]{1,0:T(8,128)S(1)} %cholesky.118), custom_call_target="Cholesky" | custom-call | tf_op jit(solution)/shard_map/jit(cholesky)/cholesky | solution.py:28
  144.9 9.8 %custom-call.16 = f32[1,128,128]{1,2,0:T(8,128)S(1)} custom-call(f32[1,128,128]{2,1,0:T(8,128)S(1)} %get-tuple-element.25), custom_call_target="InvertDiagBlocksLowerTriangular" | custom-call | tf_op jit(solution)/shard_map/jit(cholesky)/cholesky | solution.py:28
  155.2 11.7 %cholesky.105 = f32[128,128]{1,0:T(8,128)S(1)} custom-call(f32[128,128]{1,0:T(8,128)S(1)} %convolution_subtract_fusion.2), custom_call_target="Cholesky" | custom-call | tf_op jit(solution)/shard_map/jit(cholesky)/cholesky | solution.py:28
  167.0 0.7 compare_reduce_fusion
  168.9 0.8 select_select_fusion
  170.0 92.8 %all-reduce.7.cloned.1.call-done = (f32[3072,256]{1,0:T(8,128)}, f32[256,256]{1,0:T(8,128)}) async-done(((f32[3072,256]{1,0:T(8,128)}, f32[256,256]{1,0:T(8,128)}), (f32[3072,256]{1,0:T(8,128)}, f32[256,256]{1,0:T(8,128)})) %all-reduce.7.cloned.1.call-update) | async-done | bytes 3407888 | tf_op jit(solution)/shard_map/psum | solution.py:11
  262.8 13.8 %convolution_bitcast_fusion = f32[512,256]{0,1:T(8,128)} fusion(f32[3072,256]{1,0:T(8,128)} %get-tuple-element.18, f32[3072,512]{1,0:T(8,128)} %param.1), kind=kOutput, calls=%fused_computation.6 | convolution fusion | flops 4831838208 | bytes 9961472 | tf_op jit(solution)/shard_map/dot_general | solution.py:32
  276.6 2.2 copy.8
  278.8 1.0 fusion.3
  279.8 3.8 while.1
  280.4 1.3 bitcast_dynamic-update-slice_fusion.2
  282.3 1.3 bitcast_dynamic-update-slice_fusion.2
  284.3 20.5 %custom-call.17 = f32[2,128,128]{1,2,0:T(8,128)S(1)} custom-call(f32[2,128,128]{2,1,0:T(8,128)} %copy-done.1), custom_call_target="InvertDiagBlocksLowerTriangular" | custom-call | tf_op jit(solution)/shard_map/triangular_solve | solution.py:43
  304.8 58.0 %reduce-scatter.4.cloned.1.call-done = f32[16,256]{1,0:T(8,128)} async-done(((f32[512,256]{1,0:T(8,128)}), f32[16,256]{1,0:T(8,128)}) %reduce-scatter.4.cloned.1.call-update) | async-done | bytes 16400
  363.5 0.7 copy.11
  364.2 0.8 fusion.8
  365.1 1.0 convolution_subtract_fusion.1
  367.6 26.7 %all_gather.3 = f32[512,256]{1,0:T(8,128)S(1)} all-gather(f32[16,256]{1,0:T(8,128)S(1)} %pad_maximum_fusion.1), channel_id=1, replica_groups=mesh['row'=32,'col'=8] {'row'}, dimensions={0}, use_global_device_ids=true | all-gather | bytes 540672 | tf_op jit(solution)/shard_map/all_gather | solution.py:50
  394.3 9.0 %convolution_subtract_fusion = f32[3072,512]{1,0:T(8,128)} fusion(f32[3072,512]{1,0:T(8,128)} %param.1, f32[3072,256]{1,0:T(8,128)S(1)} %copy-done, f32[512,256]{1,0:T(8,128)S(1)} %all_gather.3), kind=kOutput, calls=%fused_computation.2 | convolution fusion | flops 4833411072 | bytes 16252928 | tf_op jit(solution)/shard_map/dot_general | solution.py:48
  (30 shorter events, 5.2 us)
Async XLA Ops:
  7.2 123.9 %all-reduce.5.cloned.1.call-start = ((), (), s32[]{:S(2)}) async-start(), calls=%async_computation.1 | async-start | bytes 524288 | tf_op jit(solution)/shard_map/psum | solution.py:22
  15.9 246.9 %all-reduce.7.cloned.1.call-start = ((), (), s32[]{:S(2)}) async-start(), calls=%async_computation.3 | async-start | bytes 6815744 | tf_op jit(solution)/shard_map/psum | solution.py:11
  169.7 193.1 %reduce-scatter.4.cloned.1.call-start = ((), (), s32[]{:S(2)}) async-start(), calls=%async_computation.2 | async-start | bytes 540672
  276.6 117.7 %copy-start = (f32[3072,256]{1,0:T(8,128)S(1)}, f32[3072,256]{1,0:T(8,128)}, u32[]{:S(2)}) copy-start(f32[3072,256]{1,0:T(8,128)} %get-tuple-element.18) | copy-start | bytes 9437188
  283.6 0.7 copy-start.1
Sparse Core Ops, SparseCore 0:
  16.0 114.9 all-reduce.4
  169.8 92.9 all-reduce.6
  278.9 83.8 reduce-scatter.3
where the time goes:
time: 411 us; the launch traced here: 410 us
  waiting for transfers between devices  262 us (64%)
  other arithmetic  61.6 us (15%)
  matrix products  34.6 us (8%)
  blocking collectives  26.7 us (6%)
  between operations  15.1 us (4%)
  local copies, waits for them, and re-layouts  9.21 us (2%)
    psum x1, waiting for transfers between devices, gram_total(): return lax.psum(local_gram, 'row')  111 us
    psum x1, waiting for transfers between devices, broadcast(): return lax.psum(block, axis)  92.8 us
    unnamed x4, waiting for transfers between devices  58 us
    another operation x6, other arithmetic, shards(): lower_factor = jnp.linalg.cholesky(gram_total(own_panel))  34 us
    all_gather x1, blocking collectives, shards(): lax.all_gather(coeffs, 'row', axis=0, tiled=True)  26.7 us
    another operation x4, other arithmetic, shards(): lax.linalg.triangular_solve(lower_factor, products, left_side=False, lowe...  22.1 us
    dot_general x1, matrix products, shards(): lax.dot_general(column_block, panel_cols, (((0,), (0,)), ((), ())), preci...  13.8 us
    dot_general x1, matrix products, shards(): lax.dot_general(panel_cols, lax.all_gather(coeffs, 'row', axis=0, tiled=T...  8.95 us
  transfers between devices with their start and end apart: 3, of which 3 were waited for; matrix products, arithmetic and copies ran while one was open for 7% of the time, Pallas kernels for 0%

commit v1 on v0

v1 whole, which is shorter than its diff:
```python
import functools

import jax
import jax.numpy as jnp
from jax import lax
from jax.experimental import pallas as pl
from jax.experimental.pallas import tpu as pltpu
from jax.sharding import PartitionSpec as P

PANEL = 256
PIECE = 32
CHUNK = 128
LAG = CHUNK // PIECE
TILE = 128
NB = 64
MESH = pl.DeviceIdType.MESH
F32 = jnp.float32
BF16 = jnp.bfloat16


def halves(x):
    high = x.astype(BF16)
    return high, (x - high.astype(F32)).astype(BF16)


def dot_split(left, right):
    lh, ll = halves(left)
    rh, rl = halves(right)
    return jnp.dot(
        jnp.concatenate([lh, ll, lh], axis=1),
        jnp.concatenate([rh, rh, rl], axis=0),
        preferred_element_type=F32,
    )


def dot_full(left, right, contract):
    return lax.dot_general(
        left,
        right,
        ((contract[:1], contract[1:]), ((), ())),
        precision=lax.Precision.HIGHEST,
        preferred_element_type=F32,
    )


def factor_inverse(full, work, w_buf):
    row = lax.broadcasted_iota(jnp.int32, (PANEL, PANEL), 0)
    col = lax.broadcasted_iota(jnp.int32, (PANEL, PANEL), 1)
    work[:, :PANEL] = full[:PANEL, :]
    work[:, PANEL:] = jnp.where(row == col, 1.0, 0.0).astype(F32)
    r = lax.broadcasted_iota(jnp.int32, (NB, 2 * NB), 0)
    c = lax.broadcasted_iota(jnp.int32, (NB, 2 * NB), 1)
    wide = lax.broadcasted_iota(jnp.int32, (NB, PANEL), 1)
    for b in range(PANEL // NB):
        pair = b // 2 * 2 * NB
        own, other = (0, NB) if b % 2 == 0 else (NB, 0)
        tile = work[b * NB : (b + 1) * NB, pair : pair + 2 * NB]
        x = pltpu.roll(tile, NB, 1)
        mine = jnp.logical_and(c >= own, c < own + NB)
        x = jnp.where(mine, jnp.where(c - own == r, 1.0, 0.0).astype(F32), x)
        for k in range(0, NB, 2):
            k0, k1 = other + k, other + k + 1
            col0 = jnp.broadcast_to(x[:, k0 : k0 + 1], x.shape)
            col1 = jnp.broadcast_to(x[:, k1 : k1 + 1], x.shape)
            row0 = jnp.broadcast_to(x[k : k + 1, :], x.shape)
            row1 = jnp.broadcast_to(x[k + 1 : k + 2, :], x.shape)
            p00 = jnp.broadcast_to(col0[k : k + 1, :], x.shape)
            p01 = jnp.broadcast_to(col1[k : k + 1, :], x.shape)
            p11 = jnp.broadcast_to(col1[k + 1 : k + 2, :], x.shape)
            inv0 = 1.0 / p00
            ratio = p01 * inv0
            inv1 = 1.0 / (p11 - p01 * ratio)
            f0 = jnp.where(r > k, col0 * inv0, 0.0)
            row1 = row1 - ratio * row0
            f1 = jnp.where(r > k + 1, (col1 - col0 * ratio) * inv1, 0.0)
            x = x - f0 * row0 - f1 * row1
        pivot = jnp.sum(jnp.where(c - other == r, x, 0.0), axis=1, keepdims=True)
        inverse = jnp.where(mine, x, 0.0) * (1.0 / jnp.sqrt(pivot))
        rows = dot_full(inverse, work[pair : pair + 2 * NB, :], (1, 0))
        w_buf[b * NB : (b + 1) * NB, :] = rows[:, PANEL:]
        if b < PANEL // NB - 1:
            below = jnp.where(wide >= (b + 1) * NB, rows[:, :PANEL], 0.0)
            work[...] = work[...] - dot_full(below, rows, (0, 0))


def panel_kernel(
    chips, wide, planes,
    a_hbm, p_out, c_out, t_out,
    a_buf, p_buf, acc, x_buf, s_buf, rs_buf, full, t_buf, w_buf, work,
    p_recv, up_send, down_send, w_recv, w_up, w_down,
    x_send, x_recv, rs_send, rs_recv, ag_send, ag_recv, fw_send, fw_recv, local,
):
    row, z = lax.axis_index("row"), lax.axis_index("col")
    rows, cols = a_buf.shape
    block = cols // (2 * chips)
    high = chips // wide
    chip, core = lax.div(row, 2), lax.rem(row, 2)
    cy, cx = lax.div(chip, wide), lax.rem(chip, wide)
    partner = row + 1 - 2 * core
    pieces = rows // PIECE
    steps = pieces // 2 + planes // 2 * LAG
    w_pieces = PANEL // PIECE

    reach = lambda d, n: min(d, n - d)
    offsets = sorted(
        ((dy, dx) for dy in range(high) for dx in range(wide) if dy or dx),
        key=lambda o: (reach(o[0], high) + reach(o[1], wide), o),
    )

    def there(dy, dx):
        return lax.rem(cy + dy, high) * wide + lax.rem(cx + dx, wide)

    def back(dy, dx):
        return there(high - dy, wide - dx)

    from_hbm = pltpu.make_async_copy(a_hbm, a_buf, local.at[0])
    top, half = pl.ds(0, rows // 2), pl.ds(rows // 2, rows // 2)
    load_top = pltpu.make_async_copy(a_hbm.at[top, pl.ds(0, PANEL)], p_buf.at[top, :], local.at[1])
    load_half = pltpu.make_async_copy(a_hbm.at[half, pl.ds(0, PANEL)], p_buf.at[half, :], local.at[2])

    @pl.when(z == 0)
    def _():
        load_top.start()
        load_half.start()

    from_hbm.start()

    barrier = pltpu.get_barrier_semaphore()
    around = [(row, lax.rem(z + 1, planes)), (row, lax.rem(z + planes - 1, planes)), (partner, z)]
    around += [(2 * there(*o) + core, z) for o in offsets]
    for device in around:
        pl.semaphore_signal(barrier, inc=1, device_id=device, device_id_type=MESH)
    acc[...] = jnp.zeros_like(acc)
    pl.semaphore_wait(barrier, len(around))

    def hop(i, plane, sends):
        part = pl.ds(pl.multiple_of(i * PIECE, PIECE), PIECE)
        return pltpu.make_async_remote_copy(
            src_ref=p_buf.at[part, :], dst_ref=p_buf.at[part, :],
            send_sem=sends.at[i], recv_sem=p_recv.at[i],
            device_id=(row, plane), device_id_type=MESH,
        )

    def w_hop(i, plane, sends):
        part = pl.ds(i * PIECE, PIECE)
        return pltpu.make_async_remote_copy(
            src_ref=w_buf.at[part, :], dst_ref=w_buf.at[part, :],
            send_sem=sends.at[i], recv_sem=w_recv.at[i],
            device_id=(row, plane), device_id_type=MESH,
        )

    def product(start, depth):
        part = pl.ds(start, depth)
        panel = p_buf[part, :]
        for tile in range(cols // TILE):
            out = slice(tile * TILE, (tile + 1) * TILE)
            acc[out, :] += dot_split(a_buf[part, out].T, panel)

    def product_tile(chunk, tile):
        part = pl.ds(pl.multiple_of(chunk * CHUNK, CHUNK), CHUNK)
        out = pl.ds(pl.multiple_of(tile * TILE, TILE), TILE)
        acc[out, :] += dot_split(a_buf[part, out].T, p_buf[part, :])

    last = planes - 1
    received = steps - z * LAG
    up_count = jnp.where(z < last, received - LAG, 0)
    down_count = jnp.where(z == 0, steps - LAG, jnp.where(z > 1, steps - (planes - z + 1) * LAG, 0))
    above = lax.rem(z + 1, planes)
    below = jnp.where(z == 0, last, z - 1)

    @pl.when(z == 0)
    def _():
        load_top.wait()
        load_half.wait()

        @pl.loop(0, steps - LAG)
        def _(i):
            hop(i, above, up_send).start()
            hop(pieces - 1 - i, below, down_send).start()

        from_hbm.wait()

        @pl.loop(0, rows // (2 * CHUNK))
        def _(i):
            product(pl.multiple_of(i * 2 * CHUNK, 2 * CHUNK), 2 * CHUNK)

    @pl.when(z != 0)
    def _():
        from_hbm.wait()

        @pl.loop(0, steps)
        def _(t):
            i = t - z * LAG
            j = t - (planes - z) * LAG

            @pl.when(i >= 0)
            def _():
                hop(i, above, up_send).wait_recv()

                @pl.when(i < up_count)
                def _():
                    hop(i, above, up_send).start()

            @pl.when(j >= 0)
            def _():
                hop(pieces - 1 - j, below, down_send).wait_recv()

                @pl.when(j < down_count)
                def _():
                    hop(pieces - 1 - j, below, down_send).start()

            @pl.when(i >= LAG)
            def _():
                product_tile(lax.div(i, LAG) - 1, lax.rem(i, LAG))

            @pl.when(j >= LAG)
            def _():
                product_tile(rows // CHUNK - lax.div(j, LAG), lax.rem(j, LAG))

        product(pl.multiple_of(received * PIECE - CHUNK, CHUNK), 2 * CHUNK)

    save_panel = pltpu.make_async_copy(p_buf, p_out, local.at[3])
    save_panel.start()

    def at(q, c):
        return pl.ds(pl.multiple_of((2 * q + c) * block, 8), block)

    def slot(q):
        return pl.ds(pl.multiple_of(q * block, 8), block)

    def swap(q):
        return pltpu.make_async_remote_copy(
            src_ref=acc.at[at(q, 1 - core), :], dst_ref=x_buf.at[slot(q), :],
            send_sem=x_send.at[q], recv_sem=x_recv.at[q],
            device_id=(partner, z), device_id_type=MESH,
        )

    def scatter(q, source):
        return pltpu.make_async_remote_copy(
            src_ref=s_buf.at[slot(q), :], dst_ref=rs_buf.at[slot(source), :],
            send_sem=rs_send.at[q], recv_sem=rs_recv.at[source],
            device_id=(2 * q + core, z), device_id_type=MESH,
        )

    order = offsets[::-1]
    for o in order + [(0, 0)]:
        swap(there(*o)).start()
    for o in order:
        q = there(*o)
        swap(q).wait_recv()
        s_buf[slot(q), :] = acc[at(q, core), :] + x_buf[slot(q), :]
        scatter(q, chip).start()
    swap(chip).wait_recv()
    total = acc[at(chip, core), :] + x_buf[slot(chip), :]

    @pl.when(z != 0)
    def _():
        up = z <= planes // 2
        for i in range(w_pieces):
            w_hop(i, above, w_up).wait_recv()

            @pl.when(z < planes // 2)
            def _():
                w_hop(i, above, w_up).start()

            @pl.when(z > planes // 2 + 1)
            def _():
                w_hop(i, below, w_down).start()

    for o in offsets:
        q = back(*o)
        scatter(q, q).wait_recv()
        total = total + rs_buf[slot(q), :]

    mine = at(chip, core)

    @pl.when(z == 0)
    def _():
        full[mine, :] = total

    @pl.when(z != 0)
    def _():
        top = dot_full(total, w_buf[...], (1, 1))
        t_buf[...] = top
        full[mine, :] = dot_full(top, w_buf[...], (1, 0))

    def gather(q, source):
        return pltpu.make_async_remote_copy(
            src_ref=full.at[mine, :], dst_ref=full.at[at(source, core), :],
            send_sem=ag_send.at[q], recv_sem=ag_recv.at[source],
            device_id=(2 * q + core, z), device_id_type=MESH,
        )

    def pass_on(q, c):
        return pltpu.make_async_remote_copy(
            src_ref=full.at[at(q, c), :], dst_ref=full.at[at(q, c), :],
            send_sem=fw_send.at[q], recv_sem=fw_recv.at[q],
            device_id=(partner, z), device_id_type=MESH,
        )

    for o in order:
        gather(there(*o), chip).start()
    pass_on(chip, core).start()
    for o in offsets:
        q = back(*o)
        gather(q, q).wait_recv()
        pass_on(q, core).start()
    for o in [(0, 0)] + offsets:
        pass_on(back(*o), 1 - core).wait_recv()

    for o in offsets:
        gather(there(*o), chip).wait_send()
    for o in [(0, 0)] + offsets:
        pass_on(there(*o), core).wait_send()

    @pl.when(z == 0)
    def _():
        factor_inverse(full, work, w_buf)
        for i in range(w_pieces):
            w_hop(i, above, w_up).start()
            w_hop(i, below, w_down).start()
        t_buf[...] = dot_full(full[mine, :], w_buf[...], (1, 1))
        tops = dot_full(full[...], w_buf[...], (1, 1))
        full[...] = dot_full(tops, w_buf[...], (1, 0))

    save_coeffs = pltpu.make_async_copy(full, c_out, local.at[4])
    save_top = pltpu.make_async_copy(t_buf, t_out, local.at[5])
    save_coeffs.start()
    save_top.start()

    for o in offsets:
        scatter(there(*o), chip).wait_send()
    for o in [(0, 0)] + offsets:
        swap(there(*o)).wait_send()

    @pl.loop(0, up_count)
    def _(i):
        hop(i, above, up_send).wait_send()

    @pl.loop(0, down_count)
    def _(i):
        hop(pieces - 1 - i, below, down_send).wait_send()

    @pl.when(z < planes // 2)
    def _():
        for i in range(w_pieces):
            w_hop(i, above, w_up).wait_send()

    @pl.when(jnp.logical_or(z == 0, z > planes // 2 + 1))
    def _():
        for i in range(w_pieces):
            w_hop(i, below, w_down).wait_send()

    save_panel.wait()
    save_coeffs.wait()
    save_top.wait()


def panel_step(matrix, chips, planes):
    rows, cols = matrix.shape
    block = cols // (2 * chips)
    pieces = rows // PIECE
    dma = lambda n: pltpu.SemaphoreType.DMA((n,))
    anywhere = pl.BlockSpec(memory_space=pl.ANY)
    return pl.pallas_call(
        functools.partial(panel_kernel, chips, min(4, chips), planes),
        out_shape=(
            jax.ShapeDtypeStruct((rows, PANEL), F32),
            jax.ShapeDtypeStruct((cols, PANEL), F32),
            jax.ShapeDtypeStruct((block, PANEL), F32),
        ),
        in_specs=[anywhere],
        out_specs=(anywhere, anywhere, anywhere),
        scratch_shapes=[
            pltpu.VMEM((rows, cols), F32),
            pltpu.VMEM((rows, PANEL), F32),
            pltpu.VMEM((cols, PANEL), F32),
            pltpu.VMEM((cols // 2, PANEL), F32),
            pltpu.VMEM((cols // 2, PANEL), F32),
            pltpu.VMEM((cols // 2, PANEL), F32),
            pltpu.VMEM((cols, PANEL), F32),
            pltpu.VMEM((block, PANEL), F32),
            pltpu.VMEM((PANEL, PANEL), F32),
            pltpu.VMEM((PANEL, 2 * PANEL), F32),
            dma(pieces), dma(pieces), dma(pieces),
            dma(PANEL // PIECE), dma(PANEL // PIECE), dma(PANEL // PIECE),
            dma(chips), dma(chips), dma(chips), dma(chips),
            dma(chips), dma(chips), dma(chips), dma(chips),
            dma(6),
        ],
        compiler_params=pltpu.CompilerParams(
            collective_id=0, has_side_effects=True, vmem_limit_bytes=40 << 20
        ),
        name="panel_step",
    )(matrix)


def remainder_kernel(a_ref, p_ref, c_ref, o_ref, c_split):
    @pl.when(pl.program_id(0) == 0)
    def _():
        high, low = halves(c_ref[...])
        c_split[:, :PANEL] = high
        c_split[:, PANEL : 2 * PANEL] = high
        c_split[:, 2 * PANEL :] = low

    high, low = halves(p_ref[...])
    o_ref[...] = a_ref[...] - lax.dot_general(
        jnp.concatenate([high, low, high], axis=1),
        c_split[...],
        (((1,), (1,)), ((), ())),
        preferred_element_type=F32,
    )


def remainder_step(matrix, panel, coeffs, tile=512):
    rows, cols = matrix.shape
    return pl.pallas_call(
        remainder_kernel,
        out_shape=jax.ShapeDtypeStruct((rows, cols), F32),
        grid=(rows // tile,),
        in_specs=[
            pl.BlockSpec((tile, cols), lambda i: (i, 0)),
            pl.BlockSpec((tile, PANEL), lambda i: (i, 0)),
            pl.BlockSpec((cols, PANEL), lambda i: (0, 0)),
        ],
        out_specs=pl.BlockSpec((tile, cols), lambda i: (i, 0)),
        scratch_shapes=[pltpu.VMEM((cols, 3 * PANEL), BF16)],
        compiler_params=pltpu.CompilerParams(vmem_limit_bytes=24 << 20),
        name="remainder_step",
    )(matrix, panel, coeffs)


def solution(mesh):
    chips, planes = mesh.shape["row"] // 2, mesh.shape["col"]

    def shards(matrix):
        panel, coeffs, top_rows = panel_step(matrix, chips, planes)
        return top_rows, remainder_step(matrix, panel, coeffs)

    return jax.shard_map(
        shards,
        mesh=mesh,
        in_specs=(P("row", "col"),),
        out_specs=(P(("col", "row"), None), P("row", "col")),
        check_vma=False,
    )
```

time: 411 us -> 96.1 us (0.23)
  the two profiles are of different devices: /device:TPU:33 before, /device:TPU:129 now
where the time goes in v1:
time: 96.1 us; the launch traced here: 95.9 us
  Pallas kernels  91.9 us (96%)
  local copies, waits for them, and re-layouts  3.38 us (4%)
    pallas_call x1, Pallas kernels, panel_step(): pl.pallas_call(functools.partial(panel_kernel, chips, min(4, chips), plan...  86.4 us
    pallas_call x1, Pallas kernels, remainder_step(): pl.pallas_call(remainder_kernel, out_shape=jax.ShapeDtypeStruct((rows, co...  5.49 us
    unnamed x3, local copies, waits for them, and re-layouts  3.38 us

profile of v1, /device:TPU:129, one launch (start us, length us, event | category | flops | bytes accessed | tf_op | source)
XLA Modules:
  0.0 95.9 jit_solution(6047653874830580721)
XLA Ops:
  0.6 0.0 copy-start
  0.6 2.8 %copy-done = f32[3072,512]{1,0:T(8,128)S(1)} copy-done((f32[3072,512]{1,0:T(8,128)S(1)}, f32[3072,512]{1,0:T(8,128)}, u32[]{:S(2)}) %copy-start) | copy-done | bytes 6291480
  3.4 86.4 %panel_step.1 = (f32[3072,256]{1,0:T(8,128)S(1)}, f32[512,256]{1,0:T(8,128)S(1)}, f32[16,256]{1,0:T(8,128)S(1)}) custom-call(f32[3072,512]{1,0:T(8,128)S(1)} %copy-done), custom_call_target="tpu_custom_call" | custom-call | tf_op jit(solution)/shard_map/panel_step/pallas_call | solution.py:365
  89.8 5.5 %remainder_step.1 = f32[3072,512]{1,0:T(8,128)} custom-call(f32[3072,512]{1,0:T(8,128)S(1)} %copy-done, f32[3072,256]{1,0:T(8,128)S(1)} %get-tuple-element.6.p_ref, f32[512,256]{1,0:T(8,128)S(1)} %get-tuple-element.7.c_ref), custom_call_target="tpu_custom_call" | custom-call | tf_op jit(solution)/shard_map/remainder_step/pallas_call | solution.py:417
  95.3 0.6 copy.4
Async XLA Ops:
  0.6 2.8 %copy-start = (f32[3072,512]{1,0:T(8,128)S(1)}, f32[3072,512]{1,0:T(8,128)}, u32[]{:S(2)}) copy-start(f32[3072,512]{1,0:T(8,128)} %a_ref.1) | copy-start | bytes 18874372
